TPU v7x, 32 devices: a whole 2x2x4 slice. The times are simulated.
32 devices in a mesh: group: 4 (over y, core), inner: 8 (over z, x).
Axes of the slice: x: 2, y: 2, z: 4, core: 2. Of those that a mesh axis runs over, the one named last changes fastest.
Arguments:
- grad_out: bfloat16 [4096, 2048], P(('group', 'inner')), may hold values from -4 to 4
- hidden_in: bfloat16 [4096, 2048], P(('group', 'inner')), may hold values from -6 to 6
- norm_gain: float32 [2048], replicated, may hold values from 0.5 to 1.5
- expert_ids: int32 [4096, 8], P(('group', 'inner')), may hold values from 0 to 31, all different within a row; in each aligned block of 128 rows (0 to 127, 128 to 255, ...) at most 40 rows name the same one
- gate_weights: float32 [4096, 8], P(('group', 'inner')), may hold values from 0.02 to 0.5
- gate_proj: bfloat16 [32, 2048, 768], P(('group', 'inner')), may hold values from -0.125 to 0.125
- up_proj: bfloat16 [32, 2048, 768], P(('group', 'inner')), may hold values from -0.125 to 0.125
- down_proj: bfloat16 [32, 768, 2048], P(('group', 'inner')), may hold values from -0.21875 to 0.21875
- out_proj: bfloat16 [4096, 2048], P('inner'), may hold values from -0.09375 to 0.09375
- query_rows: bfloat16 [4096, 4096], P('group', 'inner'), may hold values from -140 to 140
- key_rows: bfloat16 [4096, 4096], P('group', 'inner'), may hold values from -7 to 7
- value_rows: bfloat16 [4096, 4096], P('group', 'inner'), may hold values from -6 to 6
Outputs:
- grad_hidden: bfloat16 [4096, 2048], P(('group', 'inner'))
- grad_gate: bfloat16 [4096, 8], P(('group', 'inner'))
- grad_queries: bfloat16 [4096, 4096], P('group', 'inner')
- grad_keys: bfloat16 [4096, 4096], P('group', 'inner')
- grad_values: bfloat16 [4096, 4096], P('group', 'inner')
Inputs may be any that keep to these rules, and one draw needn't show every extreme that they name: `expert_ids`: each row names 8 different experts; in the rows of one device no expert is named more than 40 times, a bound that some block reaches.
All inputs are finite; a program needn't handle non-finite values.
Results may differ from a plain program's by a relative error of at most 0.019.
Values may be sent and summed in bfloat16 or wider, within the bound.
A program may use at most 128 MiB of HBM per device.

v0:
```python
import jax
import jax.numpy as jnp
from jax import lax
from jax.sharding import PartitionSpec as P

HD = 128
SEQS = 2


def dot_rt(left, right):
    return lax.dot_general(
        left, right, (((1,), (1,)), ((), ())), preferred_element_type=jnp.float32
    )


def dot_lt(left, right):
    return lax.dot_general(
        left, right, (((0,), (0,)), ((), ())), preferred_element_type=jnp.float32
    )


def expert_backward(arrived, gate_mat, up_mat, down_mat):
    model_width = gate_mat.shape[0]
    grad_in = arrived[:, :model_width]
    normed_in = arrived[:, model_width:]
    gate_pre = jnp.dot(normed_in, gate_mat, preferred_element_type=jnp.float32)
    up_pre = jnp.dot(normed_in, up_mat, preferred_element_type=jnp.float32)
    sigma = jax.nn.sigmoid(gate_pre)
    act = gate_pre * sigma
    slope = sigma * (1.0 + gate_pre * (1.0 - sigma))
    expert_hidden = act * up_pre
    grad_hid = dot_rt(grad_in, down_mat)
    gate_score = jnp.sum(grad_hid * expert_hidden, axis=1).astype(jnp.bfloat16)
    grad_gatepre = (grad_hid * up_pre * slope).astype(jnp.bfloat16)
    grad_uppre = (grad_hid * act).astype(jnp.bfloat16)
    pair_grad = (dot_rt(grad_gatepre, gate_mat) + dot_rt(grad_uppre, up_mat)).astype(jnp.bfloat16)
    return (pair_grad, gate_score)


def local(
    grad_out,
    hidden_in,
    norm_gain,
    expert_ids,
    gate_weights,
    gate_proj,
    up_proj,
    down_proj,
    out_proj,
    query_rows,
    key_rows,
    value_rows,
):
    tok_dev, model_width = grad_out.shape
    top_count = expert_ids.shape[1]
    groups = lax.axis_size("group")
    inner_size = lax.axis_size("inner")
    experts = groups * inner_size
    capacity = max(2, 5 * tok_dev * top_count // (4 * experts))
    local_heads = out_proj.shape[0] // HD
    length = query_rows.shape[0] // SEQS
    att_scale = HD ** (-0.5)
    causal = jnp.arange(length)[:, None] >= jnp.arange(length)[None, :]

    def by_head(matrix):
        return (
            matrix.reshape(SEQS, length, local_heads, HD)
            .transpose(0, 2, 1, 3)
            .reshape(SEQS * local_heads, length, HD)
        )

    def by_token(stacked):
        return (
            stacked.reshape(SEQS, local_heads, length, HD)
            .transpose(0, 2, 1, 3)
            .reshape(SEQS * length, local_heads * HD)
        )

    def masked_scores(query, key_part):
        return jnp.where(causal, dot_rt(query, key_part) * att_scale, -jnp.inf)

    query_items = by_head(query_rows)
    key_items = by_head(key_rows)
    value_items = by_head(value_rows)
    hid_full = hidden_in.astype(jnp.float32)
    inv_rms = lax.rsqrt(jnp.mean(hid_full * hid_full, axis=1, keepdims=True) + 1e-06)
    normal_rows = hid_full * inv_rms
    normed = (normal_rows * norm_gain).astype(jnp.bfloat16)
    flat_ids = expert_ids.reshape(-1)
    pair_count = flat_ids.shape[0]
    onehot = (flat_ids[:, None] == jnp.arange(experts, dtype=jnp.int32)[None, :]).astype(jnp.int32)
    earlier = jnp.cumsum(onehot, axis=0) - onehot
    slot_index = jnp.sum(earlier * onehot, axis=1)
    target = flat_ids * capacity + slot_index
    token_rows = jnp.concatenate([grad_out, normed], axis=1)
    blank_row = jnp.zeros((1, 2 * model_width), jnp.bfloat16)
    owner_token = (
        jnp.full((experts * capacity,), tok_dev, jnp.int32)
        .at[target]
        .set(jnp.arange(pair_count, dtype=jnp.int32) // top_count)
    )
    send_rows = jnp.concatenate([token_rows, blank_row], axis=0)
    outgoing = send_rows[owner_token]
    arrived = lax.all_to_all(
        outgoing.reshape(experts, capacity, 2 * model_width),
        ("group", "inner"),
        split_axis=0,
        concat_axis=0,
        tiled=True,
    )
    arrived = arrived.reshape(experts * capacity, 2 * model_width)
    pair_grad, gate_score = expert_backward(arrived, gate_proj[0], up_proj[0], down_proj[0])
    returned, score_back = (
        lax.all_to_all(
            pair_grad.reshape(experts, capacity, model_width),
            ("group", "inner"),
            split_axis=0,
            concat_axis=0,
            tiled=True,
        ),
        lax.all_to_all(
            gate_score.reshape(experts, capacity),
            ("group", "inner"),
            split_axis=0,
            concat_axis=0,
            tiled=True,
        ),
    )
    returned = returned.reshape(experts * capacity, model_width)[target]
    grad_gate = score_back.reshape(experts * capacity)[target].reshape(tok_dev, top_count)
    moe_grad = jnp.einsum(
        "tk,tkd->td",
        gate_weights,
        returned.reshape(tok_dev, top_count, model_width).astype(jnp.float32),
    )
    scaled = moe_grad * norm_gain
    inner_mean = jnp.mean(scaled * normal_rows, axis=1, keepdims=True)
    grad_hidden = (
        grad_out.astype(jnp.float32) + inv_rms * (scaled - normal_rows * inner_mean)
    ).astype(jnp.bfloat16)
    grad_attn = dot_rt(lax.all_gather(grad_hidden, "inner", axis=0, tiled=True), out_proj).astype(
        jnp.bfloat16
    )
    grad_items = by_head(grad_attn)

    def attend(block_item):
        query, key_part, value, grad_part = block_item
        scores = masked_scores(query, key_part)
        peak = jnp.max(scores, axis=1, keepdims=True)
        exp_scores = jnp.exp(scores - peak)
        probs = exp_scores / jnp.sum(exp_scores, axis=1, keepdims=True)
        probs_half = probs.astype(jnp.bfloat16)
        grad_v = dot_lt(probs_half, grad_part).astype(jnp.bfloat16)
        grad_probs = dot_rt(grad_part, value)
        delta = jnp.sum(probs * grad_probs, axis=1, keepdims=True)
        grad_scores = (probs * (grad_probs - delta)).astype(jnp.bfloat16)
        grad_q = (
            att_scale * jnp.dot(grad_scores, key_part, preferred_element_type=jnp.float32)
        ).astype(jnp.bfloat16)
        grad_k = (att_scale * dot_lt(grad_scores, query)).astype(jnp.bfloat16)
        return (grad_q, grad_k, grad_v)

    results = lax.map(
        lambda block_item: attend(block_item), (query_items, key_items, value_items, grad_items)
    )
    return (
        grad_hidden,
        grad_gate,
        by_token(results[0]),
        by_token(results[1]),
        by_token(results[2]),
    )


def solution(mesh):
    in_specs = (
        P(("group", "inner"), None),
        P(("group", "inner"), None),
        P(),
        P(("group", "inner"), None),
        P(("group", "inner"), None),
        P(("group", "inner"), None, None),
        P(("group", "inner"), None, None),
        P(("group", "inner"), None, None),
        P("inner", None),
        P("group", "inner"),
        P("group", "inner"),
        P("group", "inner"),
    )
    out_specs = (
        P(("group", "inner"), None),
        P(("group", "inner"), None),
        P("group", "inner"),
        P("group", "inner"),
        P("group", "inner"),
    )
    return jax.shard_map(local, mesh=mesh, in_specs=in_specs, out_specs=out_specs, check_vma=False)
```

profile of v0, /device:TPU:0, one launch (start us, length us, event | category | flops | bytes accessed | tf_op | source)
XLA Modules:
  0.0 628.6 jit_solution(9642393507748024651)
XLA Ops:
  9.0 9.0 %reduce-window.6 = s32[32,8,128]{2,1,0:T(8,128)S(1)} reduce-window(s32[32,8,128]{2,1,0:T(8,128)S(1)} %fusion.68, s32[]{:T(128)} %copy.83), window={size=1x1x128 pad=0_0x0_0x127_0}, to_apply=%region_1.0 | reduce-window | flops 4161536 | bytes 262148 | tf_op jit(solution)/shard_map/reduce-window
  18.7 4.3 scatter_custom_fusion
  25.6 2.2 fusion.56
  27.8 20.2 %gather_fusion = bf16[1280,4096]{1,0:T(8,128)(2,1)} fusion(bf16[129,4096]{1,0:T(8,128)(2,1)} %fusion.56, s32[2048]{0:T(1024)S(1)} %pad_clamp_fusion), kind=kCustom, calls=%fused_computation | custom fusion | bytes 20976640 | tf_op jit(solution)/shard_map/gather | solution.py:103
  47.9 237.0 %all_to_all.16 = bf16[32,40,4096]{2,1,0:T(8,128)(2,1)S(1)} all-to-all(bf16[32,40,4096]{2,1,0:T(8,128)(2,1)} %bitcast.146), channel_id=1, replica_groups=mesh['group'=4,'inner'=8] {'group','inner'}, dimensions={0} | all-to-all | bytes 20971520 | tf_op jit(solution)/shard_map/all_to_all | solution.py:104
  285.0 4.7 fusion.37
  289.7 6.4 %fusion.39 = f32[1280,768]{0,1:T(8,128)} fusion(bf16[1280,4096]{1,0:T(8,128)(2,1)S(1)} %bitcast.148, bf16[1,2048,768]{2,1,0:T(8,128)(2,1)S(1)} %copy-done.9), kind=kOutput, calls=%fused_computation.50 | convolution fusion | flops 4026531840 | bytes 12320768 | tf_op jit(solution)/shard_map/dot_general | solution.py:27
  296.1 7.7 %multiply_reduce_fusion.1 = (bf16[1280]{0:T(1024)(128)(2,1)S(1)}, f32[1280,768]{0,1:T(8,128)}) fusion(f32[1280,768]{0,1:T(8,128)} %fusion.39, f32[1280,768]{0,1:T(8,128)S(1)} %fusion.37, bf16[1,768,2048]{2,1,0:T(8,128)(2,1)S(1)} %copy-done.8, bf16[1280,4096]{1,0:T(8,128)(2,1)S(1)} %bitcast.149), kind=kOutput, calls=%fused_computation.54 | convolution fusion | flops 4033411840 | bytes 20187648 | tf_op jit(solution)/shard_map/dot_general | solution.py:11
  303.8 12.5 %fusion.44 = f32[1280,2048]{1,0:T(8,128)} fusion(bf16[1,2048,768]{2,1,0:T(8,128)(2,1)S(1)} %copy-done, f32[1280,768]{0,1:T(8,128)S(1)} %fusion.37, f32[1280,768]{0,1:T(8,128)} %get-tuple-element.106, f32[1280,768]{0,1:T(8,128)} %fusion.39), kind=kOutput, calls=%fused_computation.59 | convolution fusion | flops 4036362240 | bytes 25427968 | tf_op jit(solution)/shard_map/dot_general | solution.py:11
  316.3 10.3 %add_convert_fusion = bf16[1280,2048]{1,0:T(8,128)(2,1)} fusion(f32[1280,2048]{1,0:T(8,128)} %fusion.44, bf16[1,2048,768]{2,1,0:T(8,128)(2,1)S(1)} %copy-done.9, f32[1280,768]{0,1:T(8,128)} %get-tuple-element.106, f32[1280,768]{0,1:T(8,128)S(1)} %fusion.37), kind=kOutput, calls=%fused_computation.45 | convolution fusion | flops 4037672960 | bytes 26738688 | tf_op jit(solution)/shard_map/dot_general | solution.py:11
  326.7 3.7 all-to-all-start.1
  330.6 117.3 %all-to-all-done.1 = bf16[32,40,2048]{2,1,0:T(8,128)(2,1)} async-done(((bf16[32,40,2048]{2,1,0:T(8,128)(2,1)}), bf16[32,40,2048]{2,1,0:T(8,128)(2,1)}, u32[]{:S(2)}, u32[]{:S(2)}) %all-to-all-start.1) | async-done | bytes 5242912 | tf_op jit(solution)/shard_map/all_to_all | solution.py:114
  447.9 12.0 %gather_fusion.1 = bf16[1024,2048]{1,0:T(8,128)(2,1)} fusion(bf16[1280,2048]{1,0:T(8,128)(2,1)} %bitcast.10, s32[1024]{0:T(1024)S(1)} %broadcast_clamp_fusion), kind=kCustom, calls=%fused_computation.1 | custom fusion | bytes 8392704 | tf_op jit(solution)/shard_map/gather | solution.py:129
  460.0 3.6 fusion.41
  466.2 2.8 all-to-all-start.2
  476.0 6.8 %gather_fusion.2 = bf16[1024]{0:T(1024)(128)(2,1)S(1)} fusion(bf16[1280]{0:T(1024)(128)(2,1)S(1)} %reshape.157, s32[1024]{0:T(1024)S(1)} %broadcast_clamp_fusion), kind=kCustom, calls=%fused_computation.2 | custom fusion | bytes 8192 | tf_op jit(solution)/shard_map/gather | solution.py:130
  483.6 52.7 %all-gather.2.cloned.1.call-done = bf16[1024,2048]{1,0:T(8,128)(2,1)} async-done(((bf16[128,2048]{1,0:T(8,128)(2,1)}), bf16[1024,2048]{1,0:T(8,128)(2,1)}) %all-gather.2.cloned.1.call-update) | async-done | bytes 4194320 | tf_op jit(solution)/shard_map/all_gather | solution.py:141
  536.3 5.2 convolution_convert_fusion.1
  542.9 69.7 %while.15 = (s32[]{:T(128)}, bf16[8,512,128]{2,1,0:T(8,128)(2,1)}, bf16[8,512,128]{2,1,0:T(8,128)(2,1)}, bf16[8,512,128]{2,1,0:T(8,128)(2,1)}, bf16[8,512,128]{2...) while((s32[]{:T(128)}, bf16[8,512,128]{2,1,0:T(8,128)(2,1)}, ...), condition=%wide.region_11.12_spmd.clone, body=%wide.region_7.11_spmd.clone.sunk | while | flops 340589056 | bytes 10251357 | solution.py:163
  549.7 1.9 fusion.101
  593.3 1.9 fusion.101
  612.6 2.0 copy.48
  614.6 2.0 copy.49
  616.7 2.2 copy.47
  (121 shorter events, 85.6 us)
Async XLA Ops:
  7.2 277.8 %copy-start = (bf16[1,2048,768]{2,1,0:T(8,128)(2,1)S(1)}, bf16[1,2048,768]{2,1,0:T(8,128)(2,1)}, u32[]{:S(2)}) copy-start(bf16[1,2048,768]{2,1,0:T(8,128)(2,1)} %param.19) | copy-start | bytes 9437188
  285.0 4.7 copy-start.9
  289.7 6.4 %copy-start.8 = (bf16[1,768,2048]{2,1,0:T(8,128)(2,1)S(1)}, bf16[1,768,2048]{2,1,0:T(8,128)(2,1)}, u32[]{:S(2)}) copy-start(bf16[1,768,2048]{2,1,0:T(8,128)(2,1)} %param.21) | copy-start | bytes 9437188
  326.7 3.8 copy-start.7
  326.7 121.2 %all-to-all-start.1 = ((bf16[32,40,2048]{2,1,0:T(8,128)(2,1)}), bf16[32,40,2048]{2,1,0:T(8,128)(2,1)}, u32[]{:S(2)}, u32[]{:S(2)}) async-start(bf16[32,40,2048]{2,1,0:T(8,128)(2,1)} %bitcast.150), calls=%async_computation.1 | async-start | bytes 10485760 | tf_op jit(solution)/shard_map/all_to_all | solution.py:114
  330.4 205.9 %all-gather.2.cloned.1.call-start = ((), (), s32[]{:S(2)}) async-start(), calls=%async_computation.3 | async-start | bytes 4718592 | tf_op jit(solution)/shard_map/all_gather | solution.py:141
  460.0 3.6 copy-start.2
  460.0 3.6 copy-start.6
  460.0 4.0 copy-start.3
  460.0 9.1 %copy-start.4 = (bf16[1024,512]{1,0:T(8,128)(2,1)S(1)}, bf16[1024,512]{1,0:T(8,128)(2,1)}, u32[]{:S(2)}) copy-start(bf16[1024,512]{1,0:T(8,128)(2,1)} %param.23) | copy-start | bytes 3145732
  466.2 9.7 %all-to-all-start.2 = ((bf16[32,1,40]{2,1,0:T(2,128)(2,1)}), bf16[32,1,40]{2,1,0:T(2,128)(2,1)S(1)}, u32[]{:S(2)}, u32[]{:S(2)}) async-start(bf16[32,1,40]{2,1,0:T(2,128)(2,1)} %convert_element_type.78), calls=%async_computation.2 | async-start | bytes 32768 | tf_op jit(solution)/shard_map/all_to_all | solution.py:121
  469.0 4.0 copy-start.5
  616.7 5.1 copy-start.1
Sparse Core Ops, SparseCore 0:
  465.6 70.6 all-gather.1
where the time goes:
time: 630 us; the launch traced here: 629 us
  blocking collectives  237 us (38%)
  waiting for transfers between devices  171 us (27%)
  matrix products  116 us (18%)
  local copies, waits for them, and re-layouts  62.6 us (10%)
  other arithmetic  20.3 us (3%)
  between operations  14.3 us (2%)
  starting transfers between devices  6.58 us (1%)
    all_to_all x1, blocking collectives, local(): lax.all_to_all(outgoing.reshape(experts, capacity, 2 * model_width), ('gr...  237 us
    all_to_all x1, waiting for transfers between devices, local(): lax.all_to_all(pair_grad.reshape(experts, capacity, model_width), ('group...  117 us
    dot_general x20, matrix products, dot_rt(): lax.dot_general(left, right, (((1,), (1,)), ((), ())), preferred_element_...  56.2 us
    all_gather x1, waiting for transfers between devices, local(): lax.all_gather(grad_hidden, 'inner', axis=0, tiled=True)  52.7 us
    dot_general x16, matrix products, dot_lt(): lax.dot_general(left, right, (((0,), (0,)), ((), ())), preferred_element_...  30 us
    gather x1, local copies, waits for them, and re-layouts, local(): outgoing = send_rows[owner_token]  20.2 us
    dot_general x8, matrix products, attend(): jnp.dot(grad_scores, key_part, preferred_element_type=jnp.float32)  15.3 us
  transfers between devices with their start and end apart: 3, of which 3 were waited for; matrix products, arithmetic and copies ran while one was open for 2% of the time, Pallas kernels for 0%

commit v1 on v0

--- a/solution.py
+++ b/solution.py
@@ -138,9 +138,18 @@
     grad_hidden = (
         grad_out.astype(jnp.float32) + inv_rms * (scaled - normal_rows * inner_mean)
     ).astype(jnp.bfloat16)
-    grad_attn = dot_rt(lax.all_gather(grad_hidden, "inner", axis=0, tiled=True), out_proj).astype(
-        jnp.bfloat16
-    )
+    grad_attn = dot_rt(
+        jnp.concatenate(
+            lax.all_to_all(
+                jnp.stack([grad_hidden for _ in range(lax.psum(1, "inner"))]),
+                "inner",
+                split_axis=0,
+                concat_axis=0,
+            ),
+            axis=0,
+        ),
+        out_proj,
+    ).astype(jnp.bfloat16)
     grad_items = by_head(grad_attn)
 
     def attend(block_item):

time: 630 us -> 655 us (1.040)
  waiting for transfers between devices: 171 us -> 198 us
  between operations: 14.3 us -> 1.19 us
    all_to_all x0 -> x1, waiting for transfers between devices: none -> 81.4 us  [local(): lax.all_to_all(jnp.stack([grad_hidden for _ in range(lax.psum(1, 'inner')...]
    all_gather x1 -> x0, waiting for transfers between devices: 52.7 us -> none  [local(): lax.all_gather(grad_hidden, 'inner', axis=0, tiled=True)]
  transfers between devices with their start and end apart: 3 -> 3, of which waited for: 3 -> 2; matrix products, arithmetic and copies ran while one was open for 2% -> 5% of each run, Pallas kernels for 0% -> 0%
where the time goes in v1:
time: 655 us; the launch traced here: 649 us
  blocking collectives  237 us (36%)
  waiting for transfers between devices  198 us (30%)
  matrix products  116 us (18%)
  local copies, waits for them, and re-layouts  64 us (10%)
  other arithmetic  19.5 us (3%)
  starting transfers between devices  12.5 us (2%)
    all_to_all x1, blocking collectives, local(): lax.all_to_all(outgoing.reshape(experts, capacity, 2 * model_width), ('gr...  237 us
    all_to_all x1, waiting for transfers between devices, local(): lax.all_to_all(pair_grad.reshape(experts, capacity, model_width), ('group...  117 us
    all_to_all x1, waiting for transfers between devices, local(): lax.all_to_all(jnp.stack([grad_hidden for _ in range(lax.psum(1, 'inner')...  81.4 us
    dot_general x20, matrix products, dot_rt(): lax.dot_general(left, right, (((1,), (1,)), ((), ())), preferred_element_...  56.4 us
    dot_general x16, matrix products, dot_lt(): lax.dot_general(left, right, (((0,), (0,)), ((), ())), preferred_element_...  30 us
    gather x1, local copies, waits for them, and re-layouts, local(): outgoing = send_rows[owner_token]  20.2 us
    dot_general x8, matrix products, attend(): jnp.dot(grad_scores, key_part, preferred_element_type=jnp.float32)  15.3 us
  transfers between devices with their start and end apart: 3, of which 2 were waited for; matrix products, arithmetic and copies ran while one was open for 5% of the time, Pallas kernels for 0%

profile of v1, /device:TPU:0, one launch (start us, length us, event | category | flops | bytes accessed | tf_op | source)
XLA Modules:
  0.0 649.2 jit_solution(4630642554560594967)
XLA Ops:
  2.5 9.0 %reduce-window.6 = s32[32,8,128]{2,1,0:T(8,128)S(1)} reduce-window(s32[32,8,128]{2,1,0:T(8,128)S(1)} %fusion.68, s32[]{:T(128)} %copy.83), window={size=1x1x128 pad=0_0x0_0x127_0}, to_apply=%region_1.0 | reduce-window | flops 4161536 | bytes 262148 | tf_op jit(solution)/shard_map/reduce-window
  12.2 4.3 scatter_custom_fusion
  19.0 2.2 fusion.56
  21.2 20.2 %gather_fusion = bf16[1280,4096]{1,0:T(8,128)(2,1)} fusion(bf16[129,4096]{1,0:T(8,128)(2,1)} %fusion.56, s32[2048]{0:T(1024)S(1)} %pad_clamp_fusion), kind=kCustom, calls=%fused_computation | custom fusion | bytes 20976640 | tf_op jit(solution)/shard_map/gather | solution.py:103
  41.4 237.5 %all_to_all.21 = bf16[32,40,4096]{2,1,0:T(8,128)(2,1)S(1)} all-to-all(bf16[32,40,4096]{2,1,0:T(8,128)(2,1)} %bitcast.147), channel_id=1, replica_groups=mesh['group'=4,'inner'=8] {'group','inner'}, dimensions={0} | all-to-all | bytes 20971520 | tf_op jit(solution)/shard_map/all_to_all | solution.py:104
  278.9 4.7 fusion.37
  283.6 6.4 fusion.39
  290.0 7.7 %multiply_reduce_fusion.1 = (bf16[1280]{0:T(1024)(128)(2,1)S(1)}, f32[1280,768]{0,1:T(8,128)}) fusion(f32[1280,768]{0,1:T(8,128)} %fusion.39, f32[1280,768]{0,1:T(8,128)S(1)} %fusion.37, bf16[1,768,2048]{2,1,0:T(8,128)(2,1)S(1)} %copy-done.10, bf16[1280,4096]{1,0:T(8,128)(2,1)S(1)} %bitcast.150), kind=kOutput, calls=%fused_computation.54 | convolution fusion | flops 4033411840 | bytes 20187648 | tf_op jit(solution)/shard_map/dot_general | solution.py:11
  297.7 12.7 %fusion.44 = f32[1280,2048]{1,0:T(8,128)} fusion(bf16[1,2048,768]{2,1,0:T(8,128)(2,1)S(1)} %copy-done, f32[1280,768]{0,1:T(8,128)S(1)} %fusion.37, f32[1280,768]{0,1:T(8,128)} %get-tuple-element.106, f32[1280,768]{0,1:T(8,128)} %fusion.39), kind=kOutput, calls=%fused_computation.59 | convolution fusion | flops 4036362240 | bytes 25427968 | tf_op jit(solution)/shard_map/dot_general | solution.py:11
  310.4 10.3 %add_convert_fusion = bf16[1280,2048]{1,0:T(8,128)(2,1)} fusion(f32[1280,2048]{1,0:T(8,128)} %fusion.44, bf16[1,2048,768]{2,1,0:T(8,128)(2,1)S(1)} %copy-done.11, f32[1280,768]{0,1:T(8,128)} %get-tuple-element.106, f32[1280,768]{0,1:T(8,128)S(1)} %fusion.37), kind=kOutput, calls=%fused_computation.45 | convolution fusion | flops 4037672960 | bytes 26738688 | tf_op jit(solution)/shard_map/dot_general | solution.py:11
  320.7 3.7 all-to-all-start.1
  325.3 116.6 %all-to-all-done.1 = bf16[32,40,2048]{2,1,0:T(8,128)(2,1)} async-done(((bf16[32,40,2048]{2,1,0:T(8,128)(2,1)}), bf16[32,40,2048]{2,1,0:T(8,128)(2,1)}, u32[]{:S(2)}, u32[]{:S(2)}) %all-to-all-start.1) | async-done | bytes 5242912 | tf_op jit(solution)/shard_map/all_to_all | solution.py:114
  442.0 2.5 all-to-all-start.2
  444.5 12.1 %gather_fusion.1 = bf16[1024,2048]{1,0:T(8,128)(2,1)} fusion(bf16[1280,2048]{1,0:T(8,128)(2,1)} %bitcast.10, s32[1024]{0:T(1024)S(1)} %broadcast_clamp_fusion), kind=kCustom, calls=%fused_computation.1 | custom fusion | bytes 8392704 | tf_op jit(solution)/shard_map/gather | solution.py:129
  456.6 3.5 fusion.41
  461.2 2.5 stack.2
  463.7 6.2 all-to-all-start.3
  474.5 6.8 %gather_fusion.2 = bf16[1024]{0:T(1024)(128)(2,1)S(1)} fusion(bf16[1280]{0:T(1024)(128)(2,1)S(1)} %reshape.162, s32[1024]{0:T(1024)S(1)} %broadcast_clamp_fusion), kind=kCustom, calls=%fused_computation.2 | custom fusion | bytes 8192 | tf_op jit(solution)/shard_map/gather | solution.py:130
  482.0 81.4 %all-to-all-done.3 = bf16[8,128,2048]{2,1,0:T(8,128)(2,1)} async-done(((bf16[8,128,2048]{2,1,0:T(8,128)(2,1)}), bf16[8,128,2048]{2,1,0:T(8,128)(2,1)}, u32[]{:S(2)}, u32[]{:S(2)}) %all-to-all-start.3) | async-done | bytes 4194336 | tf_op jit(solution)/shard_map/all_to_all | solution.py:143
  563.4 5.2 convolution_convert_fusion.1
  570.1 69.7 %while.15 = (s32[]{:T(128)}, bf16[8,512,128]{2,1,0:T(8,128)(2,1)}, bf16[8,512,128]{2,1,0:T(8,128)(2,1)}, bf16[8,512,128]{2,1,0:T(8,128)(2,1)}, bf16[8,512,128]{2...) while((s32[]{:T(128)}, bf16[8,512,128]{2,1,0:T(8,128)(2,1)}, ...), condition=%wide.region_11.12_spmd.clone, body=%wide.region_7.11_spmd.clone.sunk | while | flops 340589056 | bytes 10251357 | solution.py:172
  639.8 2.0 copy.48
  641.8 2.0 copy.49
  643.9 2.2 copy.47
  (125 shorter events, 86.0 us)
Async XLA Ops:
  0.6 278.2 %copy-start = (bf16[1,2048,768]{2,1,0:T(8,128)(2,1)S(1)}, bf16[1,2048,768]{2,1,0:T(8,128)(2,1)}, u32[]{:S(2)}) copy-start(bf16[1,2048,768]{2,1,0:T(8,128)(2,1)} %param.19) | copy-start | bytes 9437188
  278.9 4.7 copy-start.11
  283.6 6.4 copy-start.10
  320.7 3.7 copy-start.9
  320.7 121.2 %all-to-all-start.1 = ((bf16[32,40,2048]{2,1,0:T(8,128)(2,1)}), bf16[32,40,2048]{2,1,0:T(8,128)(2,1)}, u32[]{:S(2)}, u32[]{:S(2)}) async-start(bf16[32,40,2048]{2,1,0:T(8,128)(2,1)} %bitcast.151), calls=%async_computation.1 | async-start | bytes 10485760 | tf_op jit(solution)/shard_map/all_to_all | solution.py:114
  442.0 19.2 %all-to-all-start.2 = ((bf16[32,1,40]{2,1,0:T(2,128)(2,1)}), bf16[32,1,40]{2,1,0:T(2,128)(2,1)S(1)}, u32[]{:S(2)}, u32[]{:S(2)}) async-start(bf16[32,1,40]{2,1,0:T(2,128)(2,1)} %convert_element_type.78), calls=%async_computation.2 | async-start | bytes 32768 | tf_op jit(solution)/shard_map/all_to_all | solution.py:121
  456.6 3.5 copy-start.2
  456.6 3.5 copy-start.8
  456.6 4.0 copy-start.4
  461.2 2.5 copy-start.3
  463.7 6.3 copy-start.5
  463.7 99.7 %all-to-all-start.3 = ((bf16[8,128,2048]{2,1,0:T(8,128)(2,1)}), bf16[8,128,2048]{2,1,0:T(8,128)(2,1)}, u32[]{:S(2)}, u32[]{:S(2)}) async-start(bf16[8,128,2048]{2,1,0:T(8,128)(2,1)} %stack.2), calls=%async_computation.3 | async-start | bytes 8388608 | tf_op jit(solution)/shard_map/all_to_all | solution.py:143
  469.9 1.6 copy-start.6
  470.3 2.6 copy-start.7
  643.9 5.1 copy-start.1
